TPU v7x, 128 devices: a whole 4x4x4 slice. The times are simulated.
128 devices in a mesh: row: 8 (over y, z_lo), col: 16 (over x, z_hi, core).
Axes of the slice: x: 4, y: 4, z: 4 (z_hi: 2, z_lo: 2; z = z_hi * 2 + z_lo), core: 2. Of those that a mesh axis runs over, the one named last changes fastest.
Arguments:
- eigvecs: float32 [512, 65536], P(('col', 'row')), may hold values from -6 to 6
- row_map: int32 [65536], replicated, may hold values from 0 to 65535, as said below
- reflectors: float32 [16, 512, 65536], P(None, 'col', 'row'), may hold values from -0.0234375 to 0.0234375
- panel_factor: float32 [2, 512, 512], replicated, may hold values from -4 to 4
- owners: int32 [16], replicated, may hold values from 0 to 15, each once
Outputs:
- back_vectors: float32 [512, 65536], P('col', 'row')
Inputs may be any that keep to these rules, and one draw needn't show every extreme that they name: row_map is a permutation of 0 to 65535 that moves aligned blocks of 64 rows whole, keeping the order inside a block. owners is a permutation; only its first 2 entries are read, so only those slots of reflectors are used.
All inputs are finite; a program needn't handle non-finite values.
Results may differ from a plain program's by a relative error of at most 0.0001.
Values sent between devices are 32-bit elements; how exact they have to be, the bound alone decides.
A program may use at most 128 MiB of HBM per device.

v0:
```python
import jax
import jax.numpy as jnp
from jax import lax
from jax.sharding import PartitionSpec as P

PANELS = 2
NB = 64


def from_everyone(x, axis):
    copies = jnp.broadcast_to(x, (lax.axis_size(axis), *x.shape))
    return lax.all_to_all(copies, axis, split_axis=0, concat_axis=0, tiled=True)


def taken_together(x, axis):
    return from_everyone(x, axis).sum(axis=0)


def hdot(left, right):
    return jnp.dot(left, right, precision=lax.Precision.HIGHEST, preferred_element_type=jnp.float32)


def per_device(eigvecs, row_map, reflectors, panel_factor, owners):
    row_count = lax.axis_size("row")
    eig_local = eigvecs.shape[0]
    total_rows = eigvecs.shape[1]
    local_rows = total_rows // row_count
    block_count = total_rows // NB
    block_index = row_map.reshape(block_count, NB)[:, 0] // NB
    blocked = eigvecs.reshape(eig_local, block_count, NB)
    ordered = jnp.take(blocked, block_index, axis=1).reshape(eig_local, row_count, local_rows)
    arrived = lax.all_to_all(ordered, "row", split_axis=1, concat_axis=0, tiled=True)
    current = arrived.reshape(eig_local * row_count, local_rows)
    for panel in range(PANELS):
        vectors = lax.all_gather(reflectors[owners[panel]], "col", axis=0, tiled=True)
        upper = jnp.triu(panel_factor[panel])
        project = taken_together(hdot(current, vectors.T), "row")
        scaled = hdot(project, upper.T)
        current = current - hdot(scaled, vectors)
    return current


def solution(mesh):
    placed = (P(("col", "row"), None), P(), P(None, "col", "row"), P(), P())
    return jax.shard_map(
        per_device, mesh=mesh, in_specs=placed, out_specs=P("col", "row"), check_vma=False
    )
```

profile of v0, /device:TPU:0, one launch (start us, length us, event | category | flops | bytes accessed | tf_op | source)
XLA Modules:
  0.0 297.6 jit_solution(3470367636473523635)
XLA Ops:
  6.5 1.3 fusion.26
  11.5 3.0 %constant_dynamic-slice_fusion = (f32[1,32,8192]{2,1,0:T(8,128)}, f32[1,32,8192]{2,1,0:T(8,128)}) fusion(f32[16,32,8192]{2,1,0:T(8,128)} %param.7, s32[]{:T(128)S(6)} %select_n.36, s32[]{:T(128)S(6)} %select_n.34), kind=kLoop, calls=%fused_computation.34 | loop fusion | bytes 4194312 | tf_op jit(solution)/shard_map/dynamic_slice | solution.py:35
  14.6 0.7 all-gather.7.cloned.1.call-update
  15.3 3.5 %reshape.21 = f32[4,1024,64]{2,1,0:T(8,128)} reshape(f32[4,65536]{1,0:T(4,128)} %param.5) | data formatting | bytes 2097152 | tf_op jit(solution)/shard_map/reshape | solution.py:30
  18.8 2.9 copy.15
  21.8 1.1 reshape.20
  23.6 7.9 %gather_fusion = f32[1024,4,64]{2,1,0:T(4,128)} fusion(f32[4,1024,64]{2,0,1:T(4,128)S(1)} %copy.15, s32[1024]{0:T(1024)S(1)} %broadcast_clamp_fusion), kind=kCustom, calls=%fused_computation | custom fusion | bytes 2101248 | tf_op jit(solution)/shard_map/jit(_take)/gather | solution.py:31
  31.6 1.7 copy.16
  33.3 0.7 gather.7
  34.5 0.7 copy.17
  35.2 21.1 %all_to_all.25 = f32[4,8,8192]{2,0,1:T(4,128)S(1)} all-to-all(f32[4,8,8192]{2,0,1:T(4,128)S(1)} %copy.17), channel_id=1, replica_groups=mesh['row'=8,'col'=16] {'row'}, dimensions={1} | all-to-all | bytes 2097152 | tf_op jit(solution)/shard_map/all_to_all | solution.py:32
  56.6 70.3 %all-gather.5.cloned.1.call-done = f32[1,512,8192]{2,1,0:T(8,128)} async-done(((f32[1,32,8192]{2,1,0:T(8,128)}), f32[1,512,8192]{2,1,0:T(8,128)}) %all-gather.5.cloned.1.call-update) | async-done | bytes 16777232 | tf_op jit(solution)/shard_map/all_gather | solution.py:35
  126.9 18.1 %fusion.6 = f32[32,512]{1,0:T(8,128)S(1)} fusion(f32[32,8192]{1,0:T(8,128)S(1)} %reshape.22, f32[1,512,8192]{2,1,0:T(8,128)} %all-gather.5.cloned.1.call-done), kind=kOutput, calls=%fused_computation.7 | convolution fusion | flops 1610612736 | bytes 17891328 | tf_op jit(solution)/shard_map/dot_general | solution.py:20
  145.1 0.9 broadcast_in_dim.32
  146.0 4.4 %all-to-all-start.1 = ((f32[8,32,512]{2,1,0:T(8,128)}), f32[8,32,512]{2,1,0:T(8,128)}, u32[]{:S(2)}, u32[]{:S(2)}) async-start(f32[8,32,512]{2,1,0:T(8,128)} %broadcast_in_dim.32), calls=%async_computation.1 | async-start | bytes 1048576 | tf_op jit(solution)/shard_map/all_to_all | solution.py:12
  150.3 10.0 %all-to-all-done.1 = f32[8,32,512]{2,1,0:T(8,128)} async-done(((f32[8,32,512]{2,1,0:T(8,128)}), f32[8,32,512]{2,1,0:T(8,128)}, u32[]{:S(2)}, u32[]{:S(2)}) %all-to-all-start.1) | async-done | bytes 524320 | tf_op jit(solution)/shard_map/all_to_all | solution.py:12
  160.3 1.1 reduce_sum.18
  161.4 1.2 fusion.15
  162.6 13.1 %fusion.8 = f32[32,8192]{1,0:T(8,128)S(1)} fusion(f32[32,8192]{1,0:T(8,128)S(1)} %reshape.22, f32[32,512]{1,0:T(8,128)S(1)} %fusion.15, f32[1,512,8192]{2,1,0:T(8,128)} %all-gather.5.cloned.1.call-done), kind=kOutput, calls=%fused_computation.9 | convolution fusion | flops 1610874880 | bytes 18939904 | tf_op jit(solution)/shard_map/dot_general | solution.py:20
  175.7 65.9 %all-gather.7.cloned.1.call-done = f32[1,512,8192]{2,1,0:T(8,128)} async-done(((f32[1,32,8192]{2,1,0:T(8,128)}), f32[1,512,8192]{2,1,0:T(8,128)}) %all-gather.7.cloned.1.call-update) | async-done | bytes 16777232 | tf_op jit(solution)/shard_map/all_gather | solution.py:35
  241.6 18.1 %fusion.2 = f32[32,512]{1,0:T(8,128)S(1)} fusion(f32[32,8192]{1,0:T(8,128)S(1)} %fusion.8, f32[1,512,8192]{2,1,0:T(8,128)} %all-gather.7.cloned.1.call-done), kind=kOutput, calls=%fused_computation.3 | convolution fusion | flops 1610612736 | bytes 17891328 | tf_op jit(solution)/shard_map/dot_general | solution.py:20
  259.8 14.3 %all_to_all.26 = f32[8,32,512]{2,1,0:T(8,128)S(1)} all-to-all(f32[8,32,512]{2,1,0:T(8,128)S(1)} %broadcast_in_dim.34), channel_id=1, replica_groups=mesh['row'=8,'col'=16] {'row'}, dimensions={0} | all-to-all | bytes 1048576 | tf_op jit(solution)/shard_map/all_to_all | solution.py:12
  274.2 2.4 fusion.14
  276.5 14.2 %fusion.11 = f32[32,8192]{1,0:T(8,128)} fusion(f32[32,8192]{1,0:T(8,128)S(1)} %fusion.8, f32[32,512]{1,0:T(8,128)S(1)} %fusion.14, f32[1,512,8192]{2,1,0:T(8,128)} %all-gather.7.cloned.1.call-done), kind=kOutput, calls=%fused_computation.10 | convolution fusion | flops 1610874880 | bytes 18939904 | tf_op jit(solution)/shard_map/dot_general | solution.py:20
  (15 shorter events, 1.8 us)
Async XLA Ops:
  6.5 120.4 %all-gather.5.cloned.1.call-start = ((), (), s32[]{:S(2)}) async-start(), calls=%async_computation.3 | async-start | bytes 17825792 | tf_op jit(solution)/shard_map/all_gather | solution.py:35
  14.5 227.1 %all-gather.7.cloned.1.call-start = ((), (), s32[]{:S(2)}) async-start(), calls=%async_computation.4 | async-start | bytes 17825792 | tf_op jit(solution)/shard_map/all_gather | solution.py:35
  56.6 104.8 %copy-start = (f32[2,512,512]{2,1,0:T(8,128)S(1)}, f32[2,512,512]{2,1,0:T(8,128)}, u32[]{:S(2)}) copy-start(f32[2,512,512]{2,1,0:T(8,128)} %param.8) | copy-start | bytes 6291460
  146.0 14.4 %all-to-all-start.1 = ((f32[8,32,512]{2,1,0:T(8,128)}), f32[8,32,512]{2,1,0:T(8,128)}, u32[]{:S(2)}, u32[]{:S(2)}) async-start(f32[8,32,512]{2,1,0:T(8,128)} %broadcast_in_dim.32), calls=%async_computation.1 | async-start | bytes 1048576 | tf_op jit(solution)/shard_map/all_to_all | solution.py:12
Sparse Core Ops, SparseCore 0:
  14.6 112.2 all-gather.4
  129.3 112.2 all-gather.6
where the time goes:
time: 298 us
  waiting for transfers between devices  147 us (49%)
  matrix products  67.1 us (23%)
  blocking collectives  35.4 us (12%)
  local copies, waits for them, and re-layouts  24.7 us (8%)
  between operations  17.1 us (6%)
  starting transfers between devices  4.43 us (1%)
    all_gather x2, waiting for transfers between devices, per_device(): lax.all_gather(reflectors[owners[panel]], 'col', axis=0, tiled=True)  136 us
    dot_general x6, matrix products, hdot(): jnp.dot(left, right, precision=lax.Precision.HIGHEST, preferred_element_t...  67.1 us
    all_to_all x1, blocking collectives, per_device(): lax.all_to_all(ordered, 'row', split_axis=1, concat_axis=0, tiled=True)  21.1 us
    all_to_all x1, blocking collectives, from_everyone(): return lax.all_to_all(copies, axis, split_axis=0, concat_axis=0, tiled=True)  14.3 us
    gather x3, local copies, waits for them, and re-layouts, per_device(): jnp.take(blocked, block_index, axis=1)  10.3 us
    all_to_all x1, waiting for transfers between devices, from_everyone(): return lax.all_to_all(copies, axis, split_axis=0, concat_axis=0, tiled=True)  9.99 us
    reshape x2, local copies, waits for them, and re-layouts, per_device(): blocked = eigvecs.reshape(eig_local, block_count, NB)  6.48 us
  transfers between devices with their start and end apart: 3, of which 3 were waited for; matrix products, arithmetic and copies ran while one was open for 18% of the time, Pallas kernels for 0%

commit v1 on v0

v1 whole, which is shorter than its diff:
```python
import jax
import jax.numpy as jnp
from jax import lax
from jax.sharding import PartitionSpec as P

PANELS = 2
NB = 64


def hdot(left, right):
    return jnp.dot(left, right, precision=lax.Precision.HIGHEST, preferred_element_type=jnp.float32)


def per_device(eigvecs, row_map, reflectors, panel_factor, owners):
    rows, cols = lax.axis_size("row"), lax.axis_size("col")
    eig_local, total_rows = eigvecs.shape
    piece = total_rows // (rows * cols)
    block_count = total_rows // NB
    block_index = row_map.reshape(block_count, NB)[:, 0] // NB
    block_index = block_index.reshape(rows, cols, piece // NB).transpose(1, 0, 2).reshape(block_count)
    blocked = eigvecs.reshape(eig_local, block_count, NB)
    ordered = jnp.take(blocked, block_index, axis=1).reshape(eig_local, rows * cols, piece)
    arrived = lax.all_to_all(ordered, ("col", "row"), split_axis=1, concat_axis=0, tiled=True)
    current = arrived.reshape(eig_local * rows * cols, piece)
    for panel in range(PANELS):
        mine = reflectors[owners[panel]]
        mine = mine.reshape(mine.shape[0], cols, piece)
        vectors = lax.all_to_all(mine, "col", split_axis=1, concat_axis=0, tiled=True)
        vectors = vectors.reshape(-1, piece)
        upper = jnp.triu(panel_factor[panel])
        project = lax.psum(hdot(current, vectors.T), ("row", "col"))
        scaled = hdot(project, upper.T)
        current = current - hdot(scaled, vectors)
    out = lax.all_to_all(current.reshape(cols, -1, piece), "col", split_axis=0, concat_axis=0, tiled=True)
    return out.transpose(1, 0, 2).reshape(-1, cols * piece)


def solution(mesh):
    placed = (P(("col", "row"), None), P(), P(None, "col", "row"), P(), P())
    return jax.shard_map(
        per_device, mesh=mesh, in_specs=placed, out_specs=P("col", "row"), check_vma=False
    )
```

time: 298 us -> 425 us (1.43)
  waiting for transfers between devices: 147 us -> 317 us
  matrix products: 67.1 us -> 18.7 us
  starting transfers between devices: 4.43 us -> 18.7 us
  blocking collectives: 35.4 us -> 23.9 us
    psum x0 -> x2, waiting for transfers between devices: none -> 290 us  [per_device(): project = lax.psum(hdot(current, vectors.T), ('row', 'col'))]
    all_gather x2 -> x0, waiting for transfers between devices: 136 us -> none  [per_device(): lax.all_gather(reflectors[owners[panel]], 'col', axis=0, tiled=True)]
    dot_general x6, matrix products: 67.1 us -> 18.7 us  [hdot(): jnp.dot(left, right, precision=lax.Precision.HIGHEST, preferred_element_t...]
    all_to_all x1 -> x3, waiting for transfers between devices: 9.99 us -> 27.1 us  [the longest x2 16.3 us: per_device(): lax.all_to_all(mine, 'col', split_axis=1, concat_axis=0, tiled=True)]
    all_to_all x1 -> x3, starting transfers between devices: 4.38 us -> 18.5 us  [the longest x1 11.2 us: per_device(): lax.all_to_all(ordered, ('col', 'row'), split_axis=1, concat_axis=0, tile...]
    all_to_all x2 -> x1, blocking collectives: 35.4 us -> 23.9 us  [per_device(): lax.all_to_all(current.reshape(cols, -1, piece), 'col', split_axis=0, con...]
  transfers between devices with their start and end apart: 3 -> 5, of which waited for: 3 -> 4; matrix products, arithmetic and copies ran while one was open for 18% -> 3% of each run, Pallas kernels for 0% -> 0%
where the time goes in v1:
time: 425 us; the launch traced here: 424 us
  waiting for transfers between devices  317 us (75%)
  local copies, waits for them, and re-layouts  28.4 us (7%)
  blocking collectives  23.9 us (6%)
  starting transfers between devices  18.7 us (4%)
  matrix products  18.7 us (4%)
  between operations  17.4 us (4%)
    psum x2, waiting for transfers between devices, per_device(): project = lax.psum(hdot(current, vectors.T), ('row', 'col'))  290 us
    all_to_all x1, blocking collectives, per_device(): lax.all_to_all(current.reshape(cols, -1, piece), 'col', split_axis=0, con...  23.9 us
    dot_general x6, matrix products, hdot(): jnp.dot(left, right, precision=lax.Precision.HIGHEST, preferred_element_t...  18.7 us
    all_to_all x2, waiting for transfers between devices, per_device(): lax.all_to_all(mine, 'col', split_axis=1, concat_axis=0, tiled=True)  16.3 us
    all_to_all x1, starting transfers between devices, per_device(): lax.all_to_all(ordered, ('col', 'row'), split_axis=1, concat_axis=0, tile...  11.2 us
    all_to_all x1, waiting for transfers between devices, per_device(): lax.all_to_all(ordered, ('col', 'row'), split_axis=1, concat_axis=0, tile...  10.8 us
    gather x3, local copies, waits for them, and re-layouts, per_device(): jnp.take(blocked, block_index, axis=1)  10.1 us
  transfers between devices with their start and end apart: 5, of which 4 were waited for; matrix products, arithmetic and copies ran while one was open for 3% of the time, Pallas kernels for 0%

profile of v1, /device:TPU:0, one launch (start us, length us, event | category | flops | bytes accessed | tf_op | source)
XLA Modules:
  0.0 424.0 jit_solution(1514986596999403053)
XLA Ops:
  6.5 1.2 reshape.71
  8.2 2.3 reshape.73
  10.6 2.9 copy.25
  13.6 7.9 %gather_fusion = f32[1024,4,64]{2,1,0:T(4,128)} fusion(f32[4,1024,64]{2,0,1:T(4,128)S(1)} %copy.25, s32[1024]{0:T(1024)S(1)} %broadcast_clamp_fusion), kind=kCustom, calls=%fused_computation | custom fusion | bytes 2101248 | tf_op jit(solution)/shard_map/jit(_take)/gather | solution.py:22
  21.5 1.7 copy.26
  24.2 1.6 copy.27
  25.9 11.2 %all-to-all-start = ((f32[4,128,512]{2,0,1:T(4,128)}), f32[4,128,512]{2,0,1:T(4,128)S(1)}, u32[]{:S(2)}, u32[]{:S(2)}) async-start(f32[4,128,512]{2,0,1:T(4,128)} %copy.27), calls=%async_computation | async-start | bytes 2097152 | tf_op jit(solution)/shard_map/all_to_all | solution.py:23
  41.5 1.7 constant_dynamic-slice_fusion
  43.8 1.6 copy.28
  45.3 10.8 %all-to-all-done = f32[4,128,512]{2,0,1:T(4,128)S(1)} async-done(((f32[4,128,512]{2,0,1:T(4,128)}), f32[4,128,512]{2,0,1:T(4,128)S(1)}, u32[]{:S(2)}, u32[]{:S(2)}) %all-to-all-start) | async-done | bytes 1048608 | tf_op jit(solution)/shard_map/all_to_all | solution.py:23
  56.2 3.7 all-to-all-start.1
  59.9 1.6 reshape.75
  61.5 16.3 %all-to-all-done.1 = f32[32,16,512]{2,0,1:T(8,128)S(1)} async-done(((f32[32,16,512]{2,0,1:T(8,128)}), f32[32,16,512]{2,0,1:T(8,128)S(1)}, u32[]{:S(2)}, u32[]{:S(2)}) %all-to-all-start.1) | async-done | bytes 1048608 | tf_op jit(solution)/shard_map/all_to_all | solution.py:28
  77.8 2.8 fusion.14
  81.2 1.6 copy.29
  82.9 3.7 all-to-all-start.2
  86.8 142.5 %all-reduce.3.cloned.1.call-done = f32[512,512]{1,0:T(8,128)} async-done(((f32[512,512]{1,0:T(8,128)}), f32[512,512]{1,0:T(8,128)}) %all-reduce.3.cloned.1.call-update) | async-done | bytes 1048592 | tf_op jit(solution)/shard_map/psum | solution.py:31
  229.3 3.5 fusion.1
  232.9 2.8 convolution_subtract_fusion.1
  235.7 4.1 fusion.15
  239.8 147.0 %all-reduce.5.cloned.1.call-done = f32[512,512]{1,0:T(8,128)} async-done(((f32[512,512]{1,0:T(8,128)}), f32[512,512]{1,0:T(8,128)}) %all-reduce.5.cloned.1.call-update) | async-done | bytes 1048592 | tf_op jit(solution)/shard_map/psum | solution.py:31
  386.8 3.5 fusion
  390.4 1.8 convolution_subtract_fusion
  392.2 23.9 %all_to_all.50 = f32[16,32,512]{2,1,0:T(8,128)S(1)} all-to-all(f32[16,32,512]{2,1,0:T(8,128)S(1)} %bitcast.61), channel_id=1, replica_groups=mesh['row'=8,'col'=16] {'col'}, dimensions={0} | all-to-all | bytes 2097152 | tf_op jit(solution)/shard_map/all_to_all | solution.py:34
  (32 shorter events, 4.7 us)
Async XLA Ops:
  6.5 1.7 copy-start.2
  24.2 12.8 %copy-start.3 = (s32[16]{0:T(128)S(1)}, s32[16]{0:T(128)}, u32[]{:S(2)}) copy-start(s32[16]{0:T(128)} %param.9) | copy-start | bytes 196
  25.9 30.3 %all-to-all-start = ((f32[4,128,512]{2,0,1:T(4,128)}), f32[4,128,512]{2,0,1:T(4,128)S(1)}, u32[]{:S(2)}, u32[]{:S(2)}) async-start(f32[4,128,512]{2,0,1:T(4,128)} %copy.27), calls=%async_computation | async-start | bytes 2097152 | tf_op jit(solution)/shard_map/all_to_all | solution.py:23
  56.2 3.7 copy-start.1
  56.2 21.6 %all-to-all-start.1 = ((f32[32,16,512]{2,0,1:T(8,128)}), f32[32,16,512]{2,0,1:T(8,128)S(1)}, u32[]{:S(2)}, u32[]{:S(2)}) async-start(f32[32,16,512]{2,0,1:T(8,128)} %copy.28), calls=%async_computation.1 | async-start | bytes 2097152 | tf_op jit(solution)/shard_map/all_to_all | solution.py:28
  59.9 169.5 %all-reduce.3.cloned.1.call-start = ((), (), s32[]{:S(2)}) async-start(), calls=%async_computation.4 | async-start | bytes 2097152 | tf_op jit(solution)/shard_map/psum | solution.py:31
  82.9 152.8 %all-to-all-start.2 = ((f32[32,16,512]{2,0,1:T(8,128)}), f32[32,16,512]{2,0,1:T(8,128)S(1)}, u32[]{:S(2)}, u32[]{:S(2)}) async-start(f32[32,16,512]{2,0,1:T(8,128)} %copy.29), calls=%async_computation.2 | async-start | bytes 2097152 | tf_op jit(solution)/shard_map/all_to_all | solution.py:28
  86.5 300.3 %all-reduce.5.cloned.1.call-start = ((), (), s32[]{:S(2)}) async-start(), calls=%async_computation.5 | async-start | bytes 2097152 | tf_op jit(solution)/shard_map/psum | solution.py:31
  239.8 150.6 %copy-start = (f32[512,512]{1,0:T(8,128)S(1)}, f32[512,512]{1,0:T(8,128)}, u32[]{:S(2)}) copy-start(f32[512,512]{1,0:T(8,128)} %convolution_subtract_fusion.1) | copy-start | bytes 3145732
Sparse Core Ops, SparseCore 0:
  80.7 148.5 all-reduce.2
  239.9 146.8 all-reduce.4

commit v2 on v0

v2 whole, which is shorter than its diff:
```python
import functools

import jax
import jax.numpy as jnp
from jax import lax
from jax.experimental import pallas as pl
from jax.experimental.pallas import tpu as pltpu
from jax.sharding import PartitionSpec as P

PANELS = 2
NB = 64
MESH = pl.DeviceIdType.MESH
PLANE = [(dx, dh, dl) for dx in range(4) for dh in range(2) for dl in range(2)]
PEERS = PLANE[1:]
SLAB = [(dx, dh) for dx in range(4) for dh in range(2)]


def split(value):
    high = value.astype(jnp.bfloat16)
    return high, (value - high.astype(jnp.float32)).astype(jnp.bfloat16)


def product(left, right, contract):
    dims = (((1,), (contract,)), ((), ()))
    lh, ll = left
    rh, rl = right
    dot = functools.partial(lax.dot_general, dimension_numbers=dims, preferred_element_type=jnp.float32)
    return dot(lh, rh) + (dot(lh, rl) + dot(ll, rh))


def kernel(
    tiles, odd, eig, vin, factor, out,
    zg, za, zr, zf, vr, vh, vl, wp, wr, ws, wy, ys, yr,
    own_sem, va_s, va_r, vb_s, vb_r, za_s, za_r, zb_s, zb_r, zc_s, zc_r,
    ws_s, ws_r, wy_s, wy_r, ya_s, ya_r, zo_s, zo_r,
):
    row, col = lax.axis_index("row"), lax.axis_index("col")
    y, zl = lax.div(row, 2), lax.rem(row, 2)
    x, zh, core = lax.div(col, 4), lax.rem(lax.div(col, 2), 2), lax.rem(col, 2)

    def device(dx, dy, dh, dl, dc=0):
        there = (
            lax.rem(y + dy, 4) * 2 + lax.rem(zl + dl, 2),
            lax.rem(x + dx, 4) * 4 + lax.rem(zh + dh, 2) * 2 + lax.rem(core + dc, 2),
        )
        return there

    def remote(src, dst, send, recv, there):
        return pltpu.make_async_remote_copy(
            src_ref=src, dst_ref=dst, send_sem=send, recv_sem=recv, device_id=there, device_id_type=MESH
        )

    def plane_of(dx, dh, dl):
        return lax.rem(x + dx, 4) * 4 + lax.rem(zh + dh, 2) * 2 + lax.rem(zl + dl, 2)

    def slab_of(dx, dh):
        return lax.rem(x + dx, 4) * 2 + lax.rem(zh + dh, 2)

    here, mine = plane_of(0, 0, 0), slab_of(0, 0)
    piece = zf.shape[1]

    barrier = pltpu.get_barrier_semaphore()
    for dx, dh, dl in PEERS:
        pl.semaphore_signal(barrier, inc=1, device_id=device(dx, 0, dh, dl), device_id_type=MESH)
    for dy in (1, 2, 3):
        pl.semaphore_signal(barrier, inc=1, device_id=device(0, dy, 0, 0), device_id_type=MESH)
    pl.semaphore_signal(barrier, inc=1, device_id=device(0, 0, 0, 0, 1), device_id_type=MESH)
    pl.semaphore_wait(barrier, len(PEERS) + 4)

    def vector_sends(panel):
        copies = []
        for o, (dx, dh) in enumerate(SLAB):
            there = slab_of(dx, dh)
            src = vin.at[panel, :, pl.ds(pl.multiple_of(there * piece, piece), piece)]
            if o == 0:
                copies.append(pltpu.make_async_copy(src, vr.at[panel, col], own_sem.at[panel]))
            else:
                copies.append(
                    remote(src, vr.at[panel, col], va_s.at[panel, o], va_r.at[panel, o], device(dx, 0, dh, 0))
                )
        return copies

    def start(copies):
        for copy in copies:
            copy.start()
        return copies

    vectors_out = [start(vector_sends(0))]

    lane = lax.broadcasted_iota(jnp.int32, (4, 128), 1)

    def gather(dy, target):
        yy = lax.rem(y + dy, 4)

        def body(step, carry):
            xz, low = lax.div(step, 2), lax.rem(step, 2)
            first = (yy * 2 + low) * (8 * piece // NB) + xz * (piece // NB)
            for tile in range(piece // 128):
                one, two = first + 2 * tile, first + 2 * tile + 1
                a, b = eig[tiles[one]], eig[tiles[two]]
                a = jnp.where(jnp.full((4, 128), odd[one]) == 0, a, pltpu.roll(a, 64, 1))
                b = jnp.where(jnp.full((4, 128), odd[two]) == 1, b, pltpu.roll(b, 64, 1))
                target[step, :, tile * 128 : (tile + 1) * 128] = jnp.where(lane < 64, a, b)
            return carry

        lax.fori_loop(0, 16, body, 0)

    along_y = []
    for dy in (2, 1, 3):
        gather(dy, zg.at[dy])
        along_y.append(remote(zg.at[dy], za.at[dy], za_s.at[dy], za_r.at[dy], device(0, dy, 0, 0)))
        along_y[-1].start()
    gather(0, za.at[0])
    near = [
        remote(za.at[0, plane_of(*o)], zr.at[here, 0], zb_s.at[i], zb_r.at[i], device(o[0], 0, o[1], o[2]))
        for i, o in enumerate(PEERS)
    ]
    start(near)
    for copy in along_y:
        copy.wait()
    far = [
        remote(
            za.at[pl.ds(1, 3), plane_of(*o)], zr.at[here, pl.ds(1, 3)], zc_s.at[i], zc_r.at[i],
            device(o[0], 0, o[1], o[2]),
        )
        for i, o in enumerate(PEERS)
    ]
    start(far)
    own = pltpu.make_async_copy(za.at[:, here], zr.at[here], own_sem.at[2])
    own.start()
    vectors_out.append(start(vector_sends(1)))

    def exchange(panel):
        copies = []
        for o, (dx, dh) in enumerate(SLAB):
            source = lax.rem(x + 4 - dx, 4) * 4 + lax.rem(zh + dh, 2) * 2 + core
            if o == 0:
                vectors_out[panel][0].wait()
            else:
                vectors_out[panel][o].wait_recv()
            copies.append(
                remote(
                    vr.at[panel, source], vr.at[panel, source], vb_s.at[panel, o], vb_r.at[panel, o],
                    device(0, 0, 0, 0, 1),
                )
            )
            copies[-1].start()
        return copies

    def split_vectors(panel, copies):
        for copy in copies:
            copy.wait()

        def body(step, carry):
            high, low = split(vr[panel, step])
            vh[panel, pl.ds(pl.multiple_of(step * 32, 32), 32), :] = high
            vl[panel, pl.ds(pl.multiple_of(step * 32, 32), 32), :] = low
            return carry

        lax.fori_loop(0, 16, body, 0)

    split_vectors(0, exchange(0))
    for copy in near + far + [own]:
        copy.wait()

    def assemble(step, carry):
        chip, dy = lax.div(step, 4), lax.rem(step, 4)
        rows = jnp.concatenate([zr[2 * chip, dy], zr[2 * chip + 1, dy]], axis=0)
        place = chip * 32 + lax.rem(y + 4 - dy, 4) * 8
        zf[pl.ds(pl.multiple_of(place, 8), 8), :] = rows
        return carry

    lax.fori_loop(0, 32, assemble, 0)

    pending = []
    for panel in range(PANELS):
        if panel == 1:
            split_vectors(1, exchange(1))
        wp[panel] = product(split(zf[...]), (vh[panel], vl[panel]), 1).reshape(wp.shape[1:])
        spread = start([
            remote(
                wp.at[panel, plane_of(*o)], wr.at[panel, here], ws_s.at[panel, i], ws_r.at[panel, i],
                device(o[0], 0, o[1], o[2]),
            )
            for i, o in enumerate(PEERS)
        ])
        row_i = lax.broadcasted_iota(jnp.int32, factor.shape[1:], 0)
        col_i = lax.broadcasted_iota(jnp.int32, factor.shape[1:], 1)
        upper = split(jnp.where(row_i <= col_i, factor[panel], 0.0))
        total = wp[panel, here]
        for (dx, dh, dl), copy in zip(PEERS, spread):
            copy.wait_recv()
            total = total + wr[panel, lax.rem(x + 4 - dx, 4) * 4 + lax.rem(zh + dh, 2) * 2 + lax.rem(zl + dl, 2)]
        ws[panel] = total
        across = start([
            remote(ws.at[panel], wy.at[panel, dy], wy_s.at[panel, dy], wy_r.at[panel, dy], device(0, dy, 0, 0))
            for dy in (1, 2, 3)
        ])
        for dy, copy in zip((1, 2, 3), across):
            copy.wait_recv()
            total = total + wy[panel, dy]
        scaled = product(split(total), upper, 1)
        ys[panel] = scaled
        yr[panel, here] = scaled
        shared = start([
            remote(
                ys.at[panel], yr.at[panel, here], ya_s.at[panel, i], ya_r.at[panel, i],
                device(o[0], 0, o[1], o[2]),
            )
            for i, o in enumerate(PEERS)
        ])
        for copy in shared:
            copy.wait_recv()
        whole = yr[panel].reshape(zf.shape[0], -1)
        zf[...] = zf[...] - product(split(whole), (vh[panel], vl[panel]), 0)
        pending += spread + across + shared

    result = []
    for o, (dx, dh) in enumerate(SLAB):
        there = slab_of(dx, dh)
        src = zf.at[pl.ds(pl.multiple_of(there * 32, 32), 32), :]
        dst = out.at[:, pl.ds(pl.multiple_of(mine * piece, piece), piece)]
        if o == 0:
            result.append(pltpu.make_async_copy(src, dst, own_sem.at[3]))
        else:
            result.append(remote(src, dst, zo_s.at[o], zo_r.at[o], device(dx, 0, dh, 0)))
    start(result)
    for copy in pending + [copy for sent in vectors_out for copy in sent[1:]]:
        copy.wait_send()
    for copy in result:
        copy.wait()


def per_device(eigvecs, row_map, reflectors, panel_factor, owners):
    total_rows = eigvecs.shape[1]
    local_rows = reflectors.shape[2]
    width = reflectors.shape[1]
    piece = total_rows // 64
    index = lax.slice(row_map, (0,), (total_rows,), (NB,)) // NB
    eig_tiles = eigvecs.reshape(4, total_rows // 128, 128).transpose(1, 0, 2)
    vectors = jnp.stack([lax.dynamic_index_in_dim(reflectors, owners[p], 0, False) for p in range(PANELS)])
    f32, bf16 = jnp.float32, jnp.bfloat16
    vmem, smem = pl.BlockSpec(memory_space=pltpu.VMEM), pl.BlockSpec(memory_space=pltpu.SMEM)
    half, all_width = 256, panel_factor.shape[1]
    dma = pltpu.SemaphoreType.DMA
    return pl.pallas_call(
        kernel,
        out_shape=jax.ShapeDtypeStruct((width, local_rows), f32),
        in_specs=[smem, smem, vmem, vmem, vmem],
        out_specs=vmem,
        scratch_shapes=[
            pltpu.VMEM((4, 16, 4, piece), f32),
            pltpu.VMEM((4, 16, 4, piece), f32),
            pltpu.VMEM((16, 4, 4, piece), f32),
            pltpu.VMEM((half, piece), f32),
            pltpu.VMEM((PANELS, 16, width, piece), f32),
            pltpu.VMEM((PANELS, all_width, piece), bf16),
            pltpu.VMEM((PANELS, all_width, piece), bf16),
            pltpu.VMEM((PANELS, 16, 16, all_width), f32),
            pltpu.VMEM((PANELS, 16, 16, all_width), f32),
            pltpu.VMEM((PANELS, 16, all_width), f32),
            pltpu.VMEM((PANELS, 4, 16, all_width), f32),
            pltpu.VMEM((PANELS, 16, all_width), f32),
            pltpu.VMEM((PANELS, 16, 16, all_width), f32),
            dma((4,)),
            dma((PANELS, 8)), dma((PANELS, 8)), dma((PANELS, 8)), dma((PANELS, 8)),
            dma((4,)), dma((4,)), dma((15,)), dma((15,)), dma((15,)), dma((15,)),
            dma((PANELS, 15)), dma((PANELS, 15)), dma((PANELS, 4)), dma((PANELS, 4)),
            dma((PANELS, 15)), dma((PANELS, 15)), dma((8,)), dma((8,)),
        ],
        compiler_params=pltpu.CompilerParams(
            collective_id=0, has_side_effects=True, vmem_limit_bytes=60 << 20
        ),
        name="back_transform",
    )(index // 2, index % 2, eig_tiles, vectors, panel_factor)


def solution(mesh):
    placed = (P(("col", "row"), None), P(), P(None, "col", "row"), P(), P())
    return jax.shard_map(
        per_device, mesh=mesh, in_specs=placed, out_specs=P("col", "row"), check_vma=False
    )
```

time: 298 us -> 127 us (0.43)
  waiting for transfers between devices: 147 us -> 0 us
  Pallas kernels: 0 us -> 114 us
  matrix products: 67.1 us -> 0 us
  blocking collectives: 35.4 us -> 0 us
  local copies, waits for them, and re-layouts: 24.7 us -> 6.56 us
  between operations: 17.1 us -> 3.86 us
  starting transfers between devices: 4.43 us -> 0 us
    all_gather x2 -> x0, waiting for transfers between devices: 136 us -> none  [per_device(): lax.all_gather(reflectors[owners[panel]], 'col', axis=0, tiled=True)]
    pallas_call x0 -> x1, Pallas kernels: none -> 114 us  [per_device(): pl.pallas_call(kernel, out_shape=jax.ShapeDtypeStruct((width, local_rows)...]
    dot_general x6 -> x0, matrix products: 67.1 us -> none  [hdot(): jnp.dot(left, right, precision=lax.Precision.HIGHEST, preferred_element_t...]
    all_to_all x2 -> x0, blocking collectives: 35.4 us -> none  [the longest x1 21.1 us: per_device(): lax.all_to_all(ordered, 'row', split_axis=1, concat_axis=0, tiled=True)]
    gather x3 -> x0, local copies, waits for them, and re-layouts: 10.3 us -> none  [per_device(): jnp.take(blocked, block_index, axis=1)]
    all_to_all x1 -> x0, waiting for transfers between devices: 9.99 us -> none  [from_everyone(): return lax.all_to_all(copies, axis, split_axis=0, concat_axis=0, tiled=True)]
    reshape x4 -> x0, local copies, waits for them, and re-layouts: 7.95 us -> none  [the longest x2 6.48 us: per_device(): blocked = eigvecs.reshape(eig_local, block_count, NB)]
    all_to_all x1 -> x0, starting transfers between devices: 4.38 us -> none  [from_everyone(): return lax.all_to_all(copies, axis, split_axis=0, concat_axis=0, tiled=True)]
  transfers between devices with their start and end apart: 3 -> 0, of which waited for: 3 -> 0; matrix products, arithmetic and copies ran while one was open for 18% -> 0% of each run, Pallas kernels for 0% -> 0%
where the time goes in v2:
time: 127 us; the launch traced here: 126 us
  Pallas kernels  114 us (90%)
  local copies, waits for them, and re-layouts  6.56 us (5%)
  between operations  3.86 us (3%)
  other arithmetic  2.09 us (2%)
    pallas_call x1, Pallas kernels, per_device(): pl.pallas_call(kernel, out_shape=jax.ShapeDtypeStruct((width, local_rows)...  114 us

profile of v2, /device:TPU:0, one launch (start us, length us, event | category | flops | bytes accessed | tf_op | source)
XLA Modules:
  0.0 126.2 jit_solution(9340867194533341105)
XLA Ops:
  0.0 1.4 %fusion.4 = (s32[1]{0:T(128)}, s32[1]{0:T(128)}) fusion(s32[16]{0:T(128)} %param.9), kind=kLoop, calls=%fused_computation.18 | loop fusion | bytes 16 | tf_op jit(solution)/shard_map/slice | solution.py:241
  5.2 1.7 %constant_dynamic-slice_fusion.1 = (f32[1,32,8192]{2,1,0:T(8,128)S(1)}, f32[1,32,8192]{2,1,0:T(8,128)S(1)}) fusion(f32[16,32,8192]{2,1,0:T(8,128)} %param.7, s32[]{:T(128)S(6)} %select_n.25, s32[]{:T(128)S(6)} %select_n.26), kind=kLoop, calls=%fused_computation.17 | loop fusion | bytes 4194312 | tf_op jit(solution)/shard_map/jit(dynamic_index_in_dim)/dynamic_slice | solution.py:241
  6.9 1.5 %pad_maximum_fusion.vin = f32[2,32,8192]{2,1,0:T(8,128)} fusion(f32[1,32,8192]{2,1,0:T(8,128)S(1)} %get-tuple-element.6, f32[1,32,8192]{2,1,0:T(8,128)S(1)} %get-tuple-element.5), kind=kLoop, calls=%fused_computation | loop fusion | flops 524288 | bytes 4194304 | tf_op jit(solution)/shard_map/stack | solution.py:241
  8.4 1.2 slice.9
  9.6 0.6 add_select_fusion
  10.2 113.7 %back_transform.1 = f32[32,8192]{1,0:T(8,128)} custom-call(s32[1024]{0:T(1024)} %get-tuple-element.8.tiles, s32[1024]{0:T(1024)} %get-tuple-element.7.odd, f32[512,4,128]{2,1,0:T(4,128)} %bitcast.5, f32[2,32,8192]{2,1,0:T(8,128)} %pad_maximum_fusion.vin, f32[2,512,512]{2,1,0:T(8,128)} %factor.1), custom_call_target="tpu_custom_call" | custom-call | tf_op jit(solution)/shard_map/back_transform/pallas_call | solution.py:246
  123.9 2.3 %copy.7 = f32[32,8192]{1,0:T(8,128)} copy(f32[32,8192]{1,0:T(8,128)} %back_transform.1) | data formatting | bytes 2097152

commit v3 on v2

--- a/solution.py
+++ b/solution.py
@@ -15,6 +15,38 @@
 SLAB = [(dx, dh) for dx in range(4) for dh in range(2)]
 
 
+class Copies:
+    def __init__(self):
+        self.open = []
+
+    def start(self, copies):
+        for copy in copies:
+            copy.start()
+            self.open.append([copy, copy.is_remote])
+        return copies
+
+    def arrived(self, copy):
+        for entry in self.open:
+            if entry[0] is copy:
+                if entry[1]:
+                    copy.wait_recv()
+                    entry[1] = False
+                else:
+                    copy.wait()
+                    self.open = [other for other in self.open if other is not entry]
+                return
+
+    def finish(self):
+        for copy, remote in self.open:
+            if remote:
+                copy.wait()
+            elif copy.is_remote:
+                copy.wait_send()
+            else:
+                copy.wait()
+        self.open = []
+
+
 def split(value):
     high = value.astype(jnp.bfloat16)
     return high, (value - high.astype(jnp.float32)).astype(jnp.bfloat16)
@@ -29,8 +61,8 @@
 
 
 def kernel(
-    tiles, odd, eig, vin, factor, out,
-    zg, za, zr, zf, vr, vh, vl, wp, wr, ws, wy, ys, yr,
+    rows, eig, vin, factor, out,
+    zg, za, zr, zf, vr, vh, vl, gh, gl, wp, wr, ws, wy, ys, yr,
     own_sem, va_s, va_r, vb_s, vb_r, za_s, za_r, zb_s, zb_r, zc_s, zc_r,
     ws_s, ws_r, wy_s, wy_r, ya_s, ya_r, zo_s, zo_r,
 ):
@@ -44,6 +76,9 @@
             lax.rem(x + dx, 4) * 4 + lax.rem(zh + dh, 2) * 2 + lax.rem(core + dc, 2),
         )
         return there
+
+    copies = Copies()
+    start, arrived, finish = copies.start, copies.arrived, copies.finish
 
     def remote(src, dst, send, recv, there):
         return pltpu.make_async_remote_copy(
@@ -68,22 +103,17 @@
     pl.semaphore_wait(barrier, len(PEERS) + 4)
 
     def vector_sends(panel):
-        copies = []
+        sends = []
         for o, (dx, dh) in enumerate(SLAB):
             there = slab_of(dx, dh)
             src = vin.at[panel, :, pl.ds(pl.multiple_of(there * piece, piece), piece)]
             if o == 0:
-                copies.append(pltpu.make_async_copy(src, vr.at[panel, col], own_sem.at[panel]))
+                sends.append(pltpu.make_async_copy(src, vr.at[panel, col], own_sem.at[panel]))
             else:
-                copies.append(
+                sends.append(
                     remote(src, vr.at[panel, col], va_s.at[panel, o], va_r.at[panel, o], device(dx, 0, dh, 0))
                 )
-        return copies
-
-    def start(copies):
-        for copy in copies:
-            copy.start()
-        return copies
+        return sends
 
     vectors_out = [start(vector_sends(0))]
 
@@ -97,9 +127,10 @@
             first = (yy * 2 + low) * (8 * piece // NB) + xz * (piece // NB)
             for tile in range(piece // 128):
                 one, two = first + 2 * tile, first + 2 * tile + 1
-                a, b = eig[tiles[one]], eig[tiles[two]]
-                a = jnp.where(jnp.full((4, 128), odd[one]) == 0, a, pltpu.roll(a, 64, 1))
-                b = jnp.where(jnp.full((4, 128), odd[two]) == 1, b, pltpu.roll(b, 64, 1))
+                a, b = eig[rows[one] >> 7], eig[rows[two] >> 7]
+                a_odd, b_odd = jnp.full((4, 128), rows[one] & NB), jnp.full((4, 128), rows[two] & NB)
+                a = jnp.where(a_odd == 0, a, pltpu.roll(a, 64, 1))
+                b = jnp.where(b_odd != 0, b, pltpu.roll(b, 64, 1))
                 target[step, :, tile * 128 : (tile + 1) * 128] = jnp.where(lane < 64, a, b)
             return carry
 
@@ -109,7 +140,7 @@
     for dy in (2, 1, 3):
         gather(dy, zg.at[dy])
         along_y.append(remote(zg.at[dy], za.at[dy], za_s.at[dy], za_r.at[dy], device(0, dy, 0, 0)))
-        along_y[-1].start()
+        start(along_y[-1:])
     gather(0, za.at[0])
     near = [
         remote(za.at[0, plane_of(*o)], zr.at[here, 0], zb_s.at[i], zb_r.at[i], device(o[0], 0, o[1], o[2]))
@@ -117,7 +148,7 @@
     ]
     start(near)
     for copy in along_y:
-        copy.wait()
+        arrived(copy)
     far = [
         remote(
             za.at[pl.ds(1, 3), plane_of(*o)], zr.at[here, pl.ds(1, 3)], zc_s.at[i], zc_r.at[i],
@@ -127,29 +158,24 @@
     ]
     start(far)
     own = pltpu.make_async_copy(za.at[:, here], zr.at[here], own_sem.at[2])
-    own.start()
-    vectors_out.append(start(vector_sends(1)))
+    start([own])
 
     def exchange(panel):
-        copies = []
+        passed = []
         for o, (dx, dh) in enumerate(SLAB):
             source = lax.rem(x + 4 - dx, 4) * 4 + lax.rem(zh + dh, 2) * 2 + core
-            if o == 0:
-                vectors_out[panel][0].wait()
-            else:
-                vectors_out[panel][o].wait_recv()
-            copies.append(
+            arrived(vectors_out[panel][o])
+            passed += start([
                 remote(
                     vr.at[panel, source], vr.at[panel, source], vb_s.at[panel, o], vb_r.at[panel, o],
                     device(0, 0, 0, 0, 1),
                 )
-            )
-            copies[-1].start()
-        return copies
-
-    def split_vectors(panel, copies):
-        for copy in copies:
-            copy.wait()
+            ])
+        return passed
+
+    def split_vectors(panel, passed):
+        for copy in passed:
+            arrived(copy)
 
         def body(step, carry):
             high, low = split(vr[panel, step])
@@ -161,7 +187,7 @@
 
     split_vectors(0, exchange(0))
     for copy in near + far + [own]:
-        copy.wait()
+        arrived(copy)
 
     def assemble(step, carry):
         chip, dy = lax.div(step, 4), lax.rem(step, 4)
@@ -172,11 +198,11 @@
 
     lax.fori_loop(0, 32, assemble, 0)
 
-    pending = []
+    def blocks(value):
+        return value.reshape(16, 16, value.shape[-1])
+
+    wp[0] = blocks(product(split(zf[...]), (vh[0], vl[0]), 1))
     for panel in range(PANELS):
-        if panel == 1:
-            split_vectors(1, exchange(1))
-        wp[panel] = product(split(zf[...]), (vh[panel], vl[panel]), 1).reshape(wp.shape[1:])
         spread = start([
             remote(
                 wp.at[panel, plane_of(*o)], wr.at[panel, here], ws_s.at[panel, i], ws_r.at[panel, i],
@@ -184,12 +210,16 @@
             )
             for i, o in enumerate(PEERS)
         ])
+        if panel == 0:
+            vectors_out.append(start(vector_sends(1)))
+        else:
+            zf[...] = zf[...] - product(split(yr[0].reshape(zf.shape[0], -1)), (vh[0], vl[0]), 0)
         row_i = lax.broadcasted_iota(jnp.int32, factor.shape[1:], 0)
         col_i = lax.broadcasted_iota(jnp.int32, factor.shape[1:], 1)
         upper = split(jnp.where(row_i <= col_i, factor[panel], 0.0))
         total = wp[panel, here]
         for (dx, dh, dl), copy in zip(PEERS, spread):
-            copy.wait_recv()
+            arrived(copy)
             total = total + wr[panel, lax.rem(x + 4 - dx, 4) * 4 + lax.rem(zh + dh, 2) * 2 + lax.rem(zl + dl, 2)]
         ws[panel] = total
         across = start([
@@ -197,7 +227,7 @@
             for dy in (1, 2, 3)
         ])
         for dy, copy in zip((1, 2, 3), across):
-            copy.wait_recv()
+            arrived(copy)
             total = total + wy[panel, dy]
         scaled = product(split(total), upper, 1)
         ys[panel] = scaled
@@ -209,11 +239,17 @@
             )
             for i, o in enumerate(PEERS)
         ])
+        if panel == 0:
+            split_vectors(1, exchange(1))
+            wp[1] = blocks(product(split(zf[...]), (vh[1], vl[1]), 1))
+            gh[...], gl[...] = split(product((vh[0], vl[0]), (vh[1], vl[1]), 1))
         for copy in shared:
-            copy.wait_recv()
-        whole = yr[panel].reshape(zf.shape[0], -1)
-        zf[...] = zf[...] - product(split(whole), (vh[panel], vl[panel]), 0)
-        pending += spread + across + shared
+            arrived(copy)
+        whole = split(yr[panel].reshape(zf.shape[0], -1))
+        if panel == 0:
+            wp[1] = wp[1] - blocks(product(whole, (gh[...], gl[...]), 0))
+        else:
+            zf[...] = zf[...] - product(whole, (vh[1], vl[1]), 0)
 
     result = []
     for o, (dx, dh) in enumerate(SLAB):
@@ -225,9 +261,14 @@
         else:
             result.append(remote(src, dst, zo_s.at[o], zo_r.at[o], device(dx, 0, dh, 0)))
     start(result)
-    for copy in pending + [copy for sent in vectors_out for copy in sent[1:]]:
-        copy.wait_send()
-    for copy in result:
+    finish()
+
+
+def fetch_kernel(owners, slots, out, sem):
+    copies = [pltpu.make_async_copy(slots.at[owners[p]], out.at[p], sem.at[p]) for p in range(PANELS)]
+    for copy in copies:
+        copy.start()
+    for copy in copies:
         copy.wait()
 
 
@@ -236,17 +277,25 @@
     local_rows = reflectors.shape[2]
     width = reflectors.shape[1]
     piece = total_rows // 64
-    index = lax.slice(row_map, (0,), (total_rows,), (NB,)) // NB
+    starts = lax.slice(row_map, (0,), (total_rows,), (NB,))
     eig_tiles = eigvecs.reshape(4, total_rows // 128, 128).transpose(1, 0, 2)
-    vectors = jnp.stack([lax.dynamic_index_in_dim(reflectors, owners[p], 0, False) for p in range(PANELS)])
     f32, bf16 = jnp.float32, jnp.bfloat16
     vmem, smem = pl.BlockSpec(memory_space=pltpu.VMEM), pl.BlockSpec(memory_space=pltpu.SMEM)
     half, all_width = 256, panel_factor.shape[1]
     dma = pltpu.SemaphoreType.DMA
+    vectors = pl.pallas_call(
+        fetch_kernel,
+        out_shape=jax.ShapeDtypeStruct((PANELS, width, local_rows), f32),
+        in_specs=[smem, pl.BlockSpec(memory_space=pltpu.HBM)],
+        out_specs=vmem,
+        scratch_shapes=[dma((PANELS,))],
+        compiler_params=pltpu.CompilerParams(vmem_limit_bytes=8 << 20),
+        name="fetch_slots",
+    )(owners, reflectors)
     return pl.pallas_call(
         kernel,
         out_shape=jax.ShapeDtypeStruct((width, local_rows), f32),
-        in_specs=[smem, smem, vmem, vmem, vmem],
+        in_specs=[smem, vmem, vmem, vmem],
         out_specs=vmem,
         scratch_shapes=[
             pltpu.VMEM((4, 16, 4, piece), f32),
@@ -256,6 +305,8 @@
             pltpu.VMEM((PANELS, 16, width, piece), f32),
             pltpu.VMEM((PANELS, all_width, piece), bf16),
             pltpu.VMEM((PANELS, all_width, piece), bf16),
+            pltpu.VMEM((all_width, all_width), bf16),
+            pltpu.VMEM((all_width, all_width), bf16),
             pltpu.VMEM((PANELS, 16, 16, all_width), f32),
             pltpu.VMEM((PANELS, 16, 16, all_width), f32),
             pltpu.VMEM((PANELS, 16, all_width), f32),
@@ -269,10 +320,10 @@
             dma((PANELS, 15)), dma((PANELS, 15)), dma((8,)), dma((8,)),
         ],
         compiler_params=pltpu.CompilerParams(
-            collective_id=0, has_side_effects=True, vmem_limit_bytes=60 << 20
+            collective_id=0, has_side_effects=True, vmem_limit_bytes=40 << 20
         ),
         name="back_transform",
-    )(index // 2, index % 2, eig_tiles, vectors, panel_factor)
+    )(starts, eig_tiles, vectors, panel_factor)
 
 
 def solution(mesh):

time: 127 us -> 117 us (0.921)
  Pallas kernels: 114 us -> 107 us
  between operations: 3.86 us -> 0.02 us
  local copies, waits for them, and re-layouts: 6.56 us -> 9.76 us
  other arithmetic: 2.09 us -> 0 us
    pallas_call x1, Pallas kernels: 114 us -> 106 us  [per_device(): pl.pallas_call(kernel, out_shape=jax.ShapeDtypeStruct((width, local_rows)...]
    unnamed x1 -> x9, local copies, waits for them, and re-layouts: 2.26 us -> 8.53 us
    dynamic_slice x1 -> x0, local copies, waits for them, and re-layouts: 1.69 us -> none  [per_device(): lax.dynamic_index_in_dim(reflectors, owners[p], 0, False)]
    another operation x1 -> x0, other arithmetic: 1.47 us -> none  [per_device(): jnp.stack([lax.dynamic_index_in_dim(reflectors, owners[p], 0, False) for...]
    slice x2 -> x1, local copies, waits for them, and re-layouts: 2.6 us -> 1.23 us  [per_device(): starts = lax.slice(row_map, (0,), (total_rows,), (NB,))]
where the time goes in v3:
time: 117 us; the launch traced here: 116 us
  Pallas kernels  107 us (91%)
  local copies, waits for them, and re-layouts  9.76 us (8%)
    pallas_call x1, Pallas kernels, per_device(): pl.pallas_call(kernel, out_shape=jax.ShapeDtypeStruct((width, local_rows)...  106 us
    unnamed x9, local copies, waits for them, and re-layouts  8.53 us

profile of v3, /device:TPU:0, one launch (start us, length us, event | category | flops | bytes accessed | tf_op | source)
XLA Modules:
  0.0 116.4 jit_solution(7601573132975916569)
XLA Ops:
  0.0 1.2 %slice.3.rows = s32[1024]{0:T(1024)S(1)} slice(s32[65536]{0:T(1024)} %param.6), slice={[0:65536:64]} | slice | bytes 8192 | tf_op jit(solution)/shard_map/slice | solution.py:280
  1.2 0.0 copy-start
  1.2 5.8 %copy-done = f32[16,32,8192]{2,1,0:T(8,128)S(1)} copy-done((f32[16,32,8192]{2,1,0:T(8,128)S(1)}, f32[16,32,8192]{2,1,0:T(8,128)}, u32[]{:S(2)}) %copy-start) | copy-done | bytes 16777240
  7.0 0.0 copy-start.3
  7.0 0.7 copy-done.3
  7.7 0.0 copy-start.1
  7.7 0.0 copy-start.2
  7.7 0.7 fetch_slots.1.vin
  8.4 0.9 copy-done.1
  9.2 0.3 copy-done.2
  9.5 105.9 %back_transform.1 = f32[32,8192]{1,0:T(8,128)S(1)} custom-call(s32[1024]{0:T(1024)S(1)} %slice.3.rows, f32[512,4,128]{2,1,0:T(4,128)S(1)} %bitcast.3, f32[2,32,8192]{2,1,0:T(8,128)S(1)} %fetch_slots.1.vin, f32[2,512,512]{2,1,0:T(8,128)S(1)} %copy-done.1), custom_call_target="tpu_custom_call" | custom-call | tf_op jit(solution)/shard_map/back_transform/pallas_call | solution.py:295
  115.5 1.0 copy.7
Async XLA Ops:
  1.2 5.8 %copy-start = (f32[16,32,8192]{2,1,0:T(8,128)S(1)}, f32[16,32,8192]{2,1,0:T(8,128)}, u32[]{:S(2)}) copy-start(f32[16,32,8192]{2,1,0:T(8,128)} %slots.1) | copy-start | bytes 50331652
  7.0 0.7 copy-start.3
  7.7 1.6 %copy-start.1 = (f32[2,512,512]{2,1,0:T(8,128)S(1)}, f32[2,512,512]{2,1,0:T(8,128)}, u32[]{:S(2)}) copy-start(f32[2,512,512]{2,1,0:T(8,128)} %factor.1) | copy-start | bytes 6291460
  7.7 1.9 %copy-start.2 = (f32[4,65536]{1,0:T(4,128)S(1)}, f32[4,65536]{1,0:T(4,128)}, u32[]{:S(2)}) copy-start(f32[4,65536]{1,0:T(4,128)} %param.5) | copy-start | bytes 3145732
